TPU v7x, 128 devices: a whole 4x4x4 slice. The times are simulated.
128 devices in a mesh: dp: 8 (over z, core), ctx: 16 (over x, y).
Axes of the slice: x: 4, y: 4, z: 4, core: 2. Of those that a mesh axis runs over, the one named last changes fastest.
Arguments:
- tokens: bfloat16 [32768, 2048], P(('dp', 'ctx')), parts along dimension 0, may hold values from -80 to 80
- qkv_weight: bfloat16 [2048, 3072], P('ctx'), may hold values from -0.125 to 0.125
- out_weight: bfloat16 [1024, 2048], P('ctx'), may hold values from -0.1875 to 0.1875
- prior_state: float32 [64, 128, 128], P('dp'), parts along dimension 0, may hold values from -240 to 240
- expert_ids: int32 [32768, 4], P(('dp', 'ctx')), parts along dimension 0, may hold values from 0 to 15, all different within a row; in each aligned block of 256 rows (0 to 255, 256 to 511, ...) at most 96 rows name the same one
- gate_weights: float32 [32768, 4], P(('dp', 'ctx')), parts along dimension 0, may hold values from 0.1 to 1
- expert_in: bfloat16 [16, 2048, 2048], P('ctx'), may hold values from -0.125 to 0.125
- expert_out: bfloat16 [16, 1024, 2048], P('ctx'), may hold values from -0.1875 to 0.1875
Outputs:
- layer_out: bfloat16 [32768, 2048], P(('dp', 'ctx')), parts along dimension 0
There are 8 independent parts, one for each index of `dp`. A program takes and returns all parts, laid end to end along the dimension named above; an argument that names none is the same for every part. Nothing has to cross between parts.
Inputs may be any that keep to these rules, and one draw needn't show every extreme that they name: `expert_ids`: within the 256 rows of one device no expert is named more than 96 times, and in some device's rows some expert is named exactly 96 times.
All inputs are finite; a program needn't handle non-finite values.
Results may differ from a plain program's by a relative error of at most 0.006.
Values may be sent and summed in bfloat16 or wider, within the bound.
No kernel may reach another device: no remote copies, remote signals or barrier semaphores. Data moves between devices by JAX's collectives and lax.ppermute only.
A program may use at most 128 MiB of HBM per device.

v0:
```python
import jax
import jax.numpy as jnp
from jax import lax
from jax.sharding import PartitionSpec as P

HEADS = 8
HD = 128
FF = 1024
SIDE = 4
GROUP = 4
EPSILON = 1e-05


def rms_rows(matrix):
    return matrix * lax.rsqrt(jnp.mean(matrix * matrix, axis=-1, keepdims=True) + EPSILON)


def swap_with(x, mask):
    return lax.ppermute(x, "dp", [(i, i ^ mask) for i in range(lax.axis_size("dp"))])


def shift_ctx(x, dx, dy):
    pairs = [
        (a * SIDE + b, (a + dx) % SIDE * SIDE + (b + dy) % SIDE)
        for a in range(SIDE)
        for b in range(SIDE)
    ]
    return lax.ppermute(x, "ctx", pairs)


def gather_by_exchange(x, axis):
    count = lax.axis_size(axis)
    spread = jnp.broadcast_to(x[None], (count,) + x.shape)
    return lax.all_to_all(spread, axis, split_axis=0, concat_axis=0, tiled=True)


def routing(expert_ids, gate_weights, experts, capacity):
    rows = expert_ids.shape[0]
    names = jnp.arange(experts, dtype=jnp.int32)
    hit = expert_ids[:, :, None] == names
    member = jnp.any(hit, axis=1)
    gate = jnp.sum(jnp.where(hit, gate_weights[:, :, None], 0.0), axis=1)
    order = jnp.arange(rows, dtype=jnp.int32)
    earlier = (order[:, None] > order[None, :]).astype(jnp.bfloat16)
    slot = jnp.dot(earlier, member.astype(jnp.bfloat16), preferred_element_type=jnp.float32)
    slot = jnp.where(member, slot.astype(jnp.int32), -1)
    slots = jnp.arange(capacity, dtype=jnp.int32)
    taken_out = slot.T[:, None, :] == slots[None, :, None]
    taken_back = slot[:, :, None] == slots[None, None, :]
    send = taken_out.astype(jnp.bfloat16).reshape(experts * capacity, rows)
    high = gate.astype(jnp.bfloat16)
    low = (gate - high.astype(jnp.float32)).astype(jnp.bfloat16)
    zero = jnp.zeros((), jnp.bfloat16)
    weigh = lambda g: jnp.where(taken_back, g[:, :, None], zero).reshape(rows, experts * capacity)
    return (send, jnp.concatenate([weigh(high), weigh(low)], axis=0))


def shards(
    tokens, qkv_weight, out_weight, prior_state, expert_ids, gate_weights, expert_in, expert_out
):
    rows, width = tokens.shape
    width_heads = HEADS * HD
    experts = lax.axis_size("ctx")
    capacity = 3 * rows * expert_ids.shape[1] // (2 * experts)
    own_heads = HEADS // GROUP
    own_width = own_heads * HD
    place = lax.axis_index("dp") % GROUP
    column = lax.axis_index("ctx") // SIDE
    row = lax.axis_index("ctx") % SIDE
    part = lambda n: lax.dynamic_slice_in_dim(
        qkv_weight, n * width_heads + place * own_width, own_width, axis=1
    )
    own_weight = jnp.concatenate([part(0), part(1), part(2)], axis=1)
    out_full = lax.all_gather(out_weight, "ctx", axis=0, tiled=True)
    normed = rms_rows(tokens.astype(jnp.float32)).astype(jnp.bfloat16)
    far = swap_with(normed, 2)
    near = swap_with(normed, 1)
    prior = [lax.dynamic_slice_in_dim(prior_state, place * own_heads, own_heads, axis=0)]
    for other in range(1, GROUP):
        theirs = lax.dynamic_slice_in_dim(
            prior_state, (place ^ other) * own_heads, own_heads, axis=0
        )
        prior.append(swap_with(theirs, other))
    prior = jnp.stack(prior)
    weight = gather_by_exchange(own_weight, "ctx").reshape(width, 3 * own_width)
    diagonal = swap_with(far, 1)
    everyone = jnp.concatenate([normed, near, far, diagonal], axis=0)
    send, weigh = routing(expert_ids, gate_weights, experts, capacity)
    projected = jnp.dot(everyone, weight, preferred_element_type=jnp.float32)
    split = lambda m: m.astype(jnp.bfloat16).reshape(GROUP, rows, own_heads, HD)
    queries = split(jax.nn.silu(projected[:, :own_width]))
    key_rows = split(jax.nn.silu(projected[:, own_width : 2 * own_width]))
    value_rows = split(projected[:, 2 * own_width :])
    state = jnp.einsum("jthd,jthe->jhde", key_rows, value_rows, preferred_element_type=jnp.float32)
    sent = state.astype(jnp.bfloat16)
    in_row = [shift_ctx(sent, 0, d).astype(jnp.float32) for d in range(1, SIDE)]
    total = (state + in_row[0] + in_row[1] + in_row[2]).astype(jnp.bfloat16)
    across = [shift_ctx(total, d, 0).astype(jnp.float32) for d in range(1, SIDE)]
    carried = prior
    for d in range(1, SIDE):
        carried = carried + jnp.where(row >= d, in_row[d - 1], 0.0)
        carried = carried + jnp.where(column >= d, across[d - 1], 0.0)
    scores = jnp.einsum("jthd,jshd->jhts", queries, key_rows, preferred_element_type=jnp.float32)
    order = jnp.arange(rows, dtype=jnp.int32)
    scores = jnp.where(order[:, None] >= order[None, :], scores, 0.0).astype(jnp.bfloat16)
    inside = jnp.einsum("jhts,jshe->jthe", scores, value_rows, preferred_element_type=jnp.float32)
    high = carried.astype(jnp.bfloat16)
    low = (carried - high.astype(jnp.float32)).astype(jnp.bfloat16)
    from_state = jnp.einsum(
        "jthd,jhde->jthe", queries, high, preferred_element_type=jnp.float32
    ) + jnp.einsum("jthd,jhde->jthe", queries, low, preferred_element_type=jnp.float32)
    head_normed = rms_rows(from_state + inside).astype(jnp.bfloat16)
    head_normed = head_normed.reshape(GROUP, rows, own_width)
    back = [head_normed[0]] + [swap_with(head_normed[j], j) for j in range(1, GROUP)]
    back = jnp.stack(back)
    ordered = [lax.dynamic_index_in_dim(back, b ^ place, 0, keepdims=False) for b in range(GROUP)]
    attended = jnp.dot(
        jnp.concatenate(ordered, axis=1), out_full, preferred_element_type=jnp.float32
    )
    hidden = (tokens.astype(jnp.float32) + attended).astype(jnp.bfloat16)
    moe_in = rms_rows(hidden.astype(jnp.float32)).astype(jnp.bfloat16)
    outgoing = jnp.dot(send, moe_in, preferred_element_type=jnp.float32).astype(jnp.bfloat16)
    outgoing = outgoing.reshape(experts, capacity, width)
    arrived = lax.all_to_all(outgoing, "ctx", split_axis=0, concat_axis=0, tiled=True)
    grouped = arrived.reshape(experts * capacity, width)
    gate_up = jnp.dot(grouped, expert_in[0], preferred_element_type=jnp.float32)
    middle = (jax.nn.silu(gate_up[:, :FF]) * gate_up[:, FF:]).astype(jnp.bfloat16)
    result = jnp.dot(middle, expert_out[0], preferred_element_type=jnp.float32).astype(jnp.bfloat16)
    returned = lax.all_to_all(
        result.reshape(experts, capacity, width), "ctx", split_axis=0, concat_axis=0, tiled=True
    ).reshape(experts * capacity, width)
    combined = jnp.dot(weigh, returned, preferred_element_type=jnp.float32)
    return (hidden.astype(jnp.float32) + (combined[:rows] + combined[rows:])).astype(jnp.bfloat16)


def solution(mesh):
    return jax.shard_map(
        shards,
        mesh=mesh,
        in_specs=(
            P(("dp", "ctx"), None),
            P("ctx", None),
            P("ctx", None),
            P("dp", None, None),
            P(("dp", "ctx"), None),
            P(("dp", "ctx"), None),
            P("ctx", None, None),
            P("ctx", None, None),
        ),
        out_specs=P(("dp", "ctx"), None),
        check_vma=False,
    )
```

profile of v0, /device:TPU:124, one launch (start us, length us, event | category | flops | bytes accessed | tf_op | source)
XLA Modules:
  0.0 372.2 jit_solution(13127794874098399859)
XLA Ops:
  8.2 2.1 broadcast_in_dim.77
  10.3 7.1 %all-to-all-start = ((bf16[16,128,768]{2,1,0:T(8,128)(2,1)}), bf16[16,128,768]{2,1,0:T(8,128)(2,1)}, u32[]{:S(2)}, u32[]{:S(2)}) async-start(bf16[16,128,768]{2,1,0:T(8,128)(2,1)} %broadcast_in_dim.77), calls=%async_computation | async-start | bytes 6291456 | tf_op jit(solution)/shard_map/all_to_all | solution.py:34
  18.5 23.9 %collective-permute-done.4 = bf16[256,2048]{1,0:T(8,128)(2,1)S(1)} collective-permute-done((bf16[256,2048]{1,0:T(8,128)(2,1)S(1)}, bf16[256,2048]{1,0:T(8,128)(2,1)S(1)}, u32[]{:S(2)}, u32[]{:S(2)}) %collective-permute-start.4) | collective-permute-done | bytes 1048608 | tf_op jit(solution)/shard_map/ppermute | solution.py:19
  43.4 1.8 collective-permute-done.5
  45.2 18.2 %all-to-all-done = bf16[16,128,768]{2,1,0:T(8,128)(2,1)} async-done(((bf16[16,128,768]{2,1,0:T(8,128)(2,1)}), bf16[16,128,768]{2,1,0:T(8,128)(2,1)}, u32[]{:S(2)}, u32[]{:S(2)}) %all-to-all-start) | async-done | bytes 3145760 | tf_op jit(solution)/shard_map/all_to_all | solution.py:34
  63.4 5.9 %fusion.3 = f32[1024,768]{1,0:T(8,128)S(1)} fusion(bf16[2048,768]{1,0:T(8,128)(2,1)} %bitcast.4, bf16[256,2048]{1,0:T(8,128)(2,1)} %collective-permute-done.5, bf16[256,2048]{1,0:T(8,128)(2,1)S(1)} %collective-permute-done.4, bf16[256,2048]{1,0:T(8,128)(2,1)} %copy-done.6, bf16[256,2048]{1,0:T(8,128)(2,1)S(1)} %fusion.16), kind=kOutput, calls=%fused_computation.6 | convolution fusion | flops 3238002688 | bytes 10485760 | tf_op jit(solution)/shard_map/dot_general | solution.py:89
  72.5 2.0 collective-permute-start.7
  74.5 1.9 dynamic-slice_bitcast_fusion.4
  76.4 11.1 %collective-permute-done.6 = bf16[4,2,128,128]{3,2,1,0:T(8,128)(2,1)S(1)} collective-permute-done((bf16[4,2,128,128]{3,2,1,0:T(8,128)(2,1)}, bf16[4,2,128,128]{3,2,1,0:T(8,128)(2,1)S(1)}, u32[]{:S(2)}, u32[]{:S(2)}) %collective-permute-start.6) | collective-permute-done | bytes 262176 | tf_op jit(solution)/shard_map/ppermute | solution.py:28
  89.1 8.3 %collective-permute-done.8 = bf16[4,2,128,128]{3,2,1,0:T(8,128)(2,1)} collective-permute-done((bf16[4,2,128,128]{3,2,1,0:T(8,128)(2,1)}, bf16[4,2,128,128]{3,2,1,0:T(8,128)(2,1)}, u32[]{:S(2)}, u32[]{:S(2)}) %collective-permute-start.8) | collective-permute-done | bytes 262176 | tf_op jit(solution)/shard_map/ppermute | solution.py:28
  97.4 1.9 fusion.40
  100.1 2.0 collective-permute-start.9
  103.6 5.1 %collective-permute-done.1 = f32[2,128,128]{2,1,0:T(8,128)} collective-permute-done((f32[2,128,128]{2,1,0:T(8,128)}, f32[2,128,128]{2,1,0:T(8,128)}, u32[]{:S(2)}, u32[]{:S(2)}) %collective-permute-start.1) | collective-permute-done | bytes 131104 | tf_op jit(solution)/shard_map/ppermute | solution.py:19
  110.3 1.9 collective-permute-done.9
  115.6 2.9 multiply_reduce_fusion
  122.6 3.7 collective-permute-done.13
  126.4 3.6 fusion.17
  130.0 1.9 convolution_convert_fusion
  131.9 80.6 %all_to_all.15 = bf16[16,96,2048]{2,1,0:T(8,128)(2,1)S(1)} all-to-all(bf16[16,96,2048]{2,1,0:T(8,128)(2,1)S(1)} %bitcast.54), channel_id=1, replica_groups=mesh['dp'=8,'ctx'=16] {'ctx'}, dimensions={0} | all-to-all | bytes 12582912 | tf_op jit(solution)/shard_map/all_to_all | solution.py:124
  212.5 15.7 %fusion = f32[1536,2048]{1,0:T(8,128)} fusion(bf16[1536,2048]{1,0:T(8,128)(2,1)S(1)} %bitcast.56, bf16[1,2048,2048]{2,1,0:T(8,128)(2,1)S(1)} %bitcast.66), kind=kOutput, calls=%fused_computation | convolution fusion | flops 12884901888 | bytes 27262976 | tf_op jit(solution)/shard_map/dot_general | solution.py:126
  228.2 13.7 %convolution_convert_fusion.1 = bf16[1536,2048]{1,0:T(8,128)(2,1)} fusion(bf16[1,1024,2048]{2,1,0:T(8,128)(2,1)S(1)} %copy-done.5, f32[1536,2048]{1,0:T(8,128)} %fusion), kind=kOutput, calls=%fused_computation.3 | convolution fusion | flops 6455033856 | bytes 23068672 | tf_op jit(solution)/shard_map/dot_general | solution.py:128
  241.9 7.8 %all-to-all-start.2 = ((bf16[16,96,2048]{2,1,0:T(8,128)(2,1)}), bf16[16,96,2048]{2,1,0:T(8,128)(2,1)}, u32[]{:S(2)}, u32[]{:S(2)}) async-start(bf16[16,96,2048]{2,1,0:T(8,128)(2,1)} %bitcast.55), calls=%async_computation.2 | async-start | bytes 12582912 | tf_op jit(solution)/shard_map/all_to_all | solution.py:129
  250.0 108.4 %all-to-all-done.2 = bf16[16,96,2048]{2,1,0:T(8,128)(2,1)} async-done(((bf16[16,96,2048]{2,1,0:T(8,128)(2,1)}), bf16[16,96,2048]{2,1,0:T(8,128)(2,1)}, u32[]{:S(2)}, u32[]{:S(2)}) %all-to-all-start.2) | async-done | bytes 6291488 | tf_op jit(solution)/shard_map/all_to_all | solution.py:129
  358.4 5.5 %fusion.20 = f32[512,2048]{1,0:T(8,128)S(1)} fusion(bf16[1536,2048]{1,0:T(8,128)(2,1)} %bitcast.27, bf16[256,1536]{0,1:T(8,128)(2,1)S(1)} %get-tuple-element.25, bf16[256,1536]{0,1:T(8,128)(2,1)S(1)} %get-tuple-element.24), kind=kOutput, calls=%fused_computation.30 | convolution fusion | flops 3224371200 | bytes 12058624 | tf_op jit(solution)/shard_map/dot_general | solution.py:132
  (74 shorter events, 21.7 us)
Async XLA Ops:
  6.5 119.9 %all-gather.2.cloned.1.call-start = ((), (), s32[]{:S(2)}) async-start(), calls=%async_computation.3 | async-start | bytes 4456448 | tf_op jit(solution)/shard_map/all_gather | solution.py:74
  8.2 9.2 %copy-start = (bf16[256,2048]{1,0:T(8,128)(2,1)S(1)}, bf16[256,2048]{1,0:T(8,128)(2,1)}, u32[]{:S(2)}) copy-start(bf16[256,2048]{1,0:T(8,128)(2,1)} %param.8) | copy-start | bytes 3145732
  10.3 53.1 %all-to-all-start = ((bf16[16,128,768]{2,1,0:T(8,128)(2,1)}), bf16[16,128,768]{2,1,0:T(8,128)(2,1)}, u32[]{:S(2)}, u32[]{:S(2)}) async-start(bf16[16,128,768]{2,1,0:T(8,128)(2,1)} %broadcast_in_dim.77), calls=%async_computation | async-start | bytes 6291456 | tf_op jit(solution)/shard_map/all_to_all | solution.py:34
  18.0 24.4 %collective-permute-start.4 = (bf16[256,2048]{1,0:T(8,128)(2,1)S(1)}, bf16[256,2048]{1,0:T(8,128)(2,1)S(1)}, u32[]{:S(2)}, u32[]{:S(2)}) collective-permute-start(bf16[256,2048]{1,0:T(8,128)(2,1)S(1)} %fusion.16), channel_id=1, source_target_pairs={{0,32},{16,48},{32,0},{48,16},{64,96},{80,112},{96,64},{112,80},{1... | collective-permute-start | bytes 3145736 | tf_op jit(solution)/shard_map/ppermute | solution.py:19
  18.5 23.9 %collective-permute-start.3 = (bf16[256,2048]{1,0:T(8,128)(2,1)S(1)}, bf16[256,2048]{1,0:T(8,128)(2,1)S(1)}, u32[]{:S(2)}, u32[]{:S(2)}) collective-permute-start(bf16[256,2048]{1,0:T(8,128)(2,1)S(1)} %fusion.16), channel_id=1, source_target_pairs={{0,16},{16,0},{32,48},{48,32},{64,80},{80,64},{96,112},{112,96},{1... | collective-permute-start | bytes 3145736 | tf_op jit(solution)/shard_map/ppermute | solution.py:19
  42.4 2.8 collective-permute-start.5
  70.8 31.9 %copy-start.3 = (s32[256,4]{0,1:T(4,128)S(1)}, s32[256,4]{0,1:T(4,128)}, u32[]{:S(2)}) copy-start(s32[256,4]{0,1:T(4,128)} %param.12) | copy-start | bytes 12292
  71.4 32.1 %copy-start.1 = (bf16[1024,256]{1,0:T(8,128)(2,1)S(1)}, bf16[1024,256]{1,0:T(8,128)(2,1)}, u32[]{:S(2)}) copy-start(bf16[1024,256]{1,0:T(8,128)(2,1)} %get-tuple-element.8) | copy-start | bytes 1572868
  72.5 15.0 %collective-permute-start.6 = (bf16[4,2,128,128]{3,2,1,0:T(8,128)(2,1)}, bf16[4,2,128,128]{3,2,1,0:T(8,128)(2,1)S(1)}, u32[]{:S(2)}, u32[]{:S(2)}) collective-permute-start(bf16[4,2,128,128]{3,2,1,0:T(8,128)(2,1)} %get-tuple-element.26), channel_id=1, source_target_pairs={{0,1},{1,2},{2,3},{3,0},{4,5},{5,6},{6,7},{7,4},{8,9},{9,10},{10,1... | collective-permute-start | bytes 786440 | tf_op jit(solution)/shard_map/ppermute | solution.py:28
  72.5 16.6 %collective-permute-start.7 = (bf16[4,2,128,128]{3,2,1,0:T(8,128)(2,1)}, bf16[4,2,128,128]{3,2,1,0:T(8,128)(2,1)}, u32[]{:S(2)}, u32[]{:S(2)}) collective-permute-start(bf16[4,2,128,128]{3,2,1,0:T(8,128)(2,1)} %get-tuple-element.26), channel_id=1, source_target_pairs={{0,2},{1,3},{2,0},{3,1},{4,6},{5,7},{6,4},{7,5},{8,10},{9,11},{10,... | collective-permute-start | bytes 786440 | tf_op jit(solution)/shard_map/ppermute | solution.py:28
  74.5 22.9 %collective-permute-start.8 = (bf16[4,2,128,128]{3,2,1,0:T(8,128)(2,1)}, bf16[4,2,128,128]{3,2,1,0:T(8,128)(2,1)}, u32[]{:S(2)}, u32[]{:S(2)}) collective-permute-start(bf16[4,2,128,128]{3,2,1,0:T(8,128)(2,1)} %get-tuple-element.26), channel_id=1, source_target_pairs={{0,3},{1,0},{2,1},{3,2},{4,7},{5,4},{6,5},{7,6},{8,11},{9,8},{10,9... | collective-permute-start | bytes 786440 | tf_op jit(solution)/shard_map/ppermute | solution.py:28
  76.4 26.3 %collective-permute-start = (f32[2,128,128]{2,1,0:T(8,128)S(1)}, f32[2,128,128]{2,1,0:T(8,128)}, u32[]{:S(2)}, u32[]{:S(2)}) collective-permute-start(f32[2,128,128]{2,1,0:T(8,128)S(1)} %get-tuple-element.21), channel_id=1, source_target_pairs={{0,16},{16,0},{32,48},{48,32},{64,80},{80,64},{96,112},{112,96},{1... | collective-permute-start | bytes 393224 | tf_op jit(solution)/shard_map/ppermute | solution.py:19
  99.2 10.3 %collective-permute-start.10 = (bf16[4,2,128,128]{3,2,1,0:T(8,128)(2,1)}, bf16[4,2,128,128]{3,2,1,0:T(8,128)(2,1)}, u32[]{:S(2)}, u32[]{:S(2)}) collective-permute-start(bf16[4,2,128,128]{3,2,1,0:T(8,128)(2,1)} %fusion.40), channel_id=1, source_target_pairs={{0,8},{1,9},{2,10},{3,11},{4,12},{5,13},{6,14},{7,15},{8,0},{9,1},... | collective-permute-start | bytes 786440 | tf_op jit(solution)/shard_map/ppermute | solution.py:28
  100.1 10.2 %collective-permute-start.11 = (bf16[4,2,128,128]{3,2,1,0:T(8,128)(2,1)}, bf16[4,2,128,128]{3,2,1,0:T(8,128)(2,1)}, u32[]{:S(2)}, u32[]{:S(2)}) collective-permute-start(bf16[4,2,128,128]{3,2,1,0:T(8,128)(2,1)} %fusion.40), channel_id=1, source_target_pairs={{0,12},{1,13},{2,14},{3,15},{4,0},{5,1},{6,2},{7,3},{8,4},{9,5},{1... | collective-permute-start | bytes 786440 | tf_op jit(solution)/shard_map/ppermute | solution.py:28
  100.1 12.1 %collective-permute-start.9 = (bf16[4,2,128,128]{3,2,1,0:T(8,128)(2,1)}, bf16[4,2,128,128]{3,2,1,0:T(8,128)(2,1)}, u32[]{:S(2)}, u32[]{:S(2)}) collective-permute-start(bf16[4,2,128,128]{3,2,1,0:T(8,128)(2,1)} %fusion.40), channel_id=1, source_target_pairs={{0,4},{1,5},{2,6},{3,7},{4,8},{5,9},{6,10},{7,11},{8,12},{9,13},{1... | collective-permute-start | bytes 786440 | tf_op jit(solution)/shard_map/ppermute | solution.py:28
  102.1 6.7 %collective-permute-start.1 = (f32[2,128,128]{2,1,0:T(8,128)}, f32[2,128,128]{2,1,0:T(8,128)}, u32[]{:S(2)}, u32[]{:S(2)}) collective-permute-start(f32[2,128,128]{2,1,0:T(8,128)} %get-tuple-element.23), channel_id=1, source_target_pairs={{0,32},{16,48},{32,0},{48,16},{64,96},{80,112},{96,64},{112,80},{1... | collective-permute-start | bytes 393224 | tf_op jit(solution)/shard_map/ppermute | solution.py:19
  102.7 6.1 %collective-permute-start.2 = (f32[2,128,128]{2,1,0:T(8,128)}, f32[2,128,128]{2,1,0:T(8,128)}, u32[]{:S(2)}, u32[]{:S(2)}) collective-permute-start(f32[2,128,128]{2,1,0:T(8,128)} %get-tuple-element.22), channel_id=1, source_target_pairs={{0,48},{16,32},{32,16},{48,0},{64,112},{80,96},{96,80},{112,64},{1... | collective-permute-start | bytes 393224 | tf_op jit(solution)/shard_map/ppermute | solution.py:19
  119.9 6.4 %collective-permute-start.13 = (bf16[256,256]{0,1:T(8,128)(2,1)S(1)}, bf16[256,256]{0,1:T(8,128)(2,1)S(1)}, u32[]{:S(2)}, u32[]{:S(2)}) collective-permute-start(bf16[256,256]{0,1:T(8,128)(2,1)S(1)} %bitcast.62), channel_id=1, source_target_pairs={{0,32},{16,48},{32,0},{48,16},{64,96},{80,112},{96,64},{112,80},{1... | collective-permute-start | bytes 393224 | tf_op jit(solution)/shard_map/ppermute | solution.py:19
  120.4 5.8 %collective-permute-start.14 = (bf16[256,256]{0,1:T(8,128)(2,1)S(1)}, bf16[256,256]{0,1:T(8,128)(2,1)S(1)}, u32[]{:S(2)}, u32[]{:S(2)}) collective-permute-start(bf16[256,256]{0,1:T(8,128)(2,1)S(1)} %bitcast.60), channel_id=1, source_target_pairs={{0,48},{16,32},{32,16},{48,0},{64,112},{80,96},{96,80},{112,64},{1... | collective-permute-start | bytes 393224 | tf_op jit(solution)/shard_map/ppermute | solution.py:19
  120.4 5.8 %collective-permute-start.12 = (bf16[256,256]{0,1:T(8,128)(2,1)S(1)}, bf16[256,256]{0,1:T(8,128)(2,1)S(1)}, u32[]{:S(2)}, u32[]{:S(2)}) collective-permute-start(bf16[256,256]{0,1:T(8,128)(2,1)S(1)} %bitcast.58), channel_id=1, source_target_pairs={{0,16},{16,0},{32,48},{48,32},{64,80},{80,64},{96,112},{112,96},{1... | collective-permute-start | bytes 393224 | tf_op jit(solution)/shard_map/ppermute | solution.py:19
  130.0 82.5 %slice-start = ((s8[8388608]{0:T(1024)(128)(4,1)}), s8[4194304]{0:T(1024)(128)(4,1)S(1)}, s32[]{:S(2)}) async-start(s8[8388608]{0:T(1024)(128)(4,1)} %bitcast.65), calls=%async_computation.4 | async-start | bytes 8388608
  131.9 80.6 %slice-start.1 = ((s8[8388608]{0:T(1024)(128)(4,1)}), s8[4194304]{0:T(1024)(128)(4,1)S(1)}, s32[]{:S(2)}) async-start(s8[8388608]{0:T(1024)(128)(4,1)} %bitcast.65), calls=%async_computation.5 | async-start | bytes 8388608
  212.5 15.7 %copy-start.5 = (bf16[1,1024,2048]{2,1,0:T(8,128)(2,1)S(1)}, bf16[1,1024,2048]{2,1,0:T(8,128)(2,1)}, u32[]{:S(2)}) copy-start(bf16[1,1024,2048]{2,1,0:T(8,128)(2,1)} %param.15) | copy-start | bytes 12582916
  241.9 116.5 %all-to-all-start.2 = ((bf16[16,96,2048]{2,1,0:T(8,128)(2,1)}), bf16[16,96,2048]{2,1,0:T(8,128)(2,1)}, u32[]{:S(2)}, u32[]{:S(2)}) async-start(bf16[16,96,2048]{2,1,0:T(8,128)(2,1)} %bitcast.55), calls=%async_computation.2 | async-start | bytes 12582912 | tf_op jit(solution)/shard_map/all_to_all | solution.py:129
  (3 other events, 10.5 us)
Sparse Core Ops, SparseCore 0:
  9.5 89.8 all-gather.1
where the time goes:
time: 373 us; the launch traced here: 372 us
  waiting for transfers between devices  186 us (50%)
  blocking collectives  80.6 us (22%)
  matrix products  52.1 us (14%)
  starting transfers between devices  23.1 us (6%)
  between operations  13.7 us (4%)
  other arithmetic  9.66 us (3%)
  local copies, waits for them, and re-layouts  6.84 us (2%)
    all_to_all x1, waiting for transfers between devices, shards(): lax.all_to_all(result.reshape(experts, capacity, width), 'ctx', split_axi...  108 us
    all_to_all x1, blocking collectives, shards(): lax.all_to_all(outgoing, 'ctx', split_axis=0, concat_axis=0, tiled=True)  80.6 us
    ppermute x9, waiting for transfers between devices, swap_with(): lax.ppermute(x, 'dp', [(i, i ^ mask) for i in range(lax.axis_size('dp'))])  34.6 us
    ppermute x6, waiting for transfers between devices, shift_ctx(): return lax.ppermute(x, 'ctx', pairs)  24.3 us
    all_to_all x1, waiting for transfers between devices, gather_by_exchange(): return lax.all_to_all(spread, axis, split_axis=0, concat_axis=0, tiled=True)  18.2 us
    dot_general x1, matrix products, shards(): gate_up = jnp.dot(grouped, expert_in[0], preferred_element_type=jnp.float32)  15.7 us
    dot_general x1, matrix products, shards(): jnp.dot(middle, expert_out[0], preferred_element_type=jnp.float32)  13.7 us
    all_to_all x1, starting transfers between devices, shards(): lax.all_to_all(result.reshape(experts, capacity, width), 'ctx', split_axi...  7.81 us
  transfers between devices with their start and end apart: 18, of which 12 were waited for; matrix products, arithmetic and copies ran while one was open for 7% of the time, Pallas kernels for 0%

commit v1 on v0

--- a/solution.py
+++ b/solution.py
@@ -9,6 +9,29 @@
 SIDE = 4
 GROUP = 4
 EPSILON = 1e-05
+
+
+def in_blocks(shard, dim, count):
+    lengths = shard.shape
+    pieces = shard.reshape(*lengths[:dim], count, lengths[dim] // count, *lengths[dim + 1 :])
+    return jnp.moveaxis(pieces, dim, 0)
+
+
+def in_order(tiles, dim):
+    tiles = jnp.moveaxis(tiles, 0, dim)
+    dims = tiles.shape
+    return tiles.reshape(*dims[:dim], dims[dim] * dims[dim + 1], *dims[dim + 2 :])
+
+
+def swapped_with_each(shard, axis, split_dim, concat_dim):
+    length, index = (lax.axis_size(axis), lax.axis_index(axis))
+    blocks = in_blocks(shard, split_dim, length)
+    gathered = [blocks[index]]
+    for step in range(1, length):
+        sent = blocks[index ^ step]
+        gathered.append(lax.ppermute(sent, axis, [(i, i ^ step) for i in range(length)]))
+    blocks = jnp.stack(gathered)[index ^ jnp.arange(length)]
+    return in_order(blocks, concat_dim)
 
 
 def rms_rows(matrix):
@@ -121,7 +144,7 @@
     moe_in = rms_rows(hidden.astype(jnp.float32)).astype(jnp.bfloat16)
     outgoing = jnp.dot(send, moe_in, preferred_element_type=jnp.float32).astype(jnp.bfloat16)
     outgoing = outgoing.reshape(experts, capacity, width)
-    arrived = lax.all_to_all(outgoing, "ctx", split_axis=0, concat_axis=0, tiled=True)
+    arrived = swapped_with_each(outgoing, "ctx", 0, 0)
     grouped = arrived.reshape(experts * capacity, width)
     gate_up = jnp.dot(grouped, expert_in[0], preferred_element_type=jnp.float32)
     middle = (jax.nn.silu(gate_up[:, :FF]) * gate_up[:, FF:]).astype(jnp.bfloat16)

time: 373 us -> 421 us (1.13)
  blocking collectives: 80.6 us -> 0 us
  waiting for transfers between devices: 186 us -> 264 us
  starting transfers between devices: 23.1 us -> 55.1 us
  local copies, waits for them, and re-layouts: 6.84 us -> 26.8 us
    all_to_all x1 -> x0, blocking collectives: 80.6 us -> none  [shards(): lax.all_to_all(outgoing, 'ctx', split_axis=0, concat_axis=0, tiled=True)]
    ppermute x0 -> x15, waiting for transfers between devices: none -> 77.4 us  [swapped_with_each(): lax.ppermute(sent, axis, [(i, i ^ step) for i in range(length)])]
    ppermute x0 -> x15, starting transfers between devices: none -> 32.7 us  [swapped_with_each(): lax.ppermute(sent, axis, [(i, i ^ step) for i in range(length)])]
    unnamed x18 -> x24, local copies, waits for them, and re-layouts: 1.01 us -> 12 us
    gather x0 -> x1, local copies, waits for them, and re-layouts: none -> 6.35 us  [swapped_with_each(): blocks = jnp.stack(gathered)[index ^ jnp.arange(length)]]
    dot_general x1, matrix products: 13.7 us -> 8.66 us  [shards(): jnp.dot(middle, expert_out[0], preferred_element_type=jnp.float32)]
  transfers between devices with their start and end apart: 18 -> 33, of which waited for: 12 -> 22; matrix products, arithmetic and copies ran while one was open for 7% -> 9% of each run, Pallas kernels for 0% -> 0%
where the time goes in v1:
time: 421 us; the launch traced here: 418 us
  waiting for transfers between devices  264 us (63%)
  starting transfers between devices  55.1 us (13%)
  matrix products  49.1 us (12%)
  local copies, waits for them, and re-layouts  26.8 us (6%)
  between operations  13.9 us (3%)
  other arithmetic  8.86 us (2%)
    all_to_all x1, waiting for transfers between devices, shards(): lax.all_to_all(result.reshape(experts, capacity, width), 'ctx', split_axi...  109 us
    ppermute x15, waiting for transfers between devices, swapped_with_each(): lax.ppermute(sent, axis, [(i, i ^ step) for i in range(length)])  77.4 us
    ppermute x9, waiting for transfers between devices, swap_with(): lax.ppermute(x, 'dp', [(i, i ^ mask) for i in range(lax.axis_size('dp'))])  34.5 us
    ppermute x15, starting transfers between devices, swapped_with_each(): lax.ppermute(sent, axis, [(i, i ^ step) for i in range(length)])  32.7 us
    ppermute x6, waiting for transfers between devices, shift_ctx(): return lax.ppermute(x, 'ctx', pairs)  24.3 us
    all_to_all x1, waiting for transfers between devices, gather_by_exchange(): return lax.all_to_all(spread, axis, split_axis=0, concat_axis=0, tiled=True)  18.2 us
    dot_general x1, matrix products, shards(): gate_up = jnp.dot(grouped, expert_in[0], preferred_element_type=jnp.float32)  17.6 us
    unnamed x24, local copies, waits for them, and re-layouts  12 us
  transfers between devices with their start and end apart: 33, of which 22 were waited for; matrix products, arithmetic and copies ran while one was open for 9% of the time, Pallas kernels for 0%

profile of v1, /device:TPU:124, one launch (start us, length us, event | category | flops | bytes accessed | tf_op | source)
XLA Modules:
  0.0 417.7 jit_solution(535788925579273158)
XLA Ops:
  10.3 7.1 %all-to-all-start = ((bf16[16,128,768]{2,1,0:T(8,128)(2,1)}), bf16[16,128,768]{2,1,0:T(8,128)(2,1)}, u32[]{:S(2)}, u32[]{:S(2)}) async-start(bf16[16,128,768]{2,1,0:T(8,128)(2,1)} %broadcast_in_dim.78), calls=%async_computation | async-start | bytes 6291456 | tf_op jit(solution)/shard_map/all_to_all | solution.py:57
  18.5 23.9 %collective-permute-done.4 = bf16[256,2048]{1,0:T(8,128)(2,1)S(1)} collective-permute-done((bf16[256,2048]{1,0:T(8,128)(2,1)S(1)}, bf16[256,2048]{1,0:T(8,128)(2,1)S(1)}, u32[]{:S(2)}, u32[]{:S(2)}) %collective-permute-start.4) | collective-permute-done | bytes 1048608 | tf_op jit(solution)/shard_map/ppermute | solution.py:42
  45.2 18.2 %all-to-all-done = bf16[16,128,768]{2,1,0:T(8,128)(2,1)} async-done(((bf16[16,128,768]{2,1,0:T(8,128)(2,1)}), bf16[16,128,768]{2,1,0:T(8,128)(2,1)}, u32[]{:S(2)}, u32[]{:S(2)}) %all-to-all-start) | async-done | bytes 3145760 | tf_op jit(solution)/shard_map/all_to_all | solution.py:57
  63.4 5.9 %fusion.3 = f32[1024,768]{1,0:T(8,128)S(1)} fusion(bf16[2048,768]{1,0:T(8,128)(2,1)} %bitcast.4, bf16[256,2048]{1,0:T(8,128)(2,1)} %collective-permute-done.5, bf16[256,2048]{1,0:T(8,128)(2,1)S(1)} %collective-permute-done.4, bf16[256,2048]{1,0:T(8,128)(2,1)} %copy-done.4, bf16[256,2048]{1,0:T(8,128)(2,1)S(1)} %fusion.16), kind=kOutput, calls=%fused_computation.7 | convolution fusion | flops 3238002688 | bytes 10485760 | tf_op jit(solution)/shard_map/dot_general | solution.py:112
  75.6 11.1 %collective-permute-done.6 = bf16[4,2,128,128]{3,2,1,0:T(8,128)(2,1)S(1)} collective-permute-done((bf16[4,2,128,128]{3,2,1,0:T(8,128)(2,1)}, bf16[4,2,128,128]{3,2,1,0:T(8,128)(2,1)S(1)}, u32[]{:S(2)}, u32[]{:S(2)}) %collective-permute-start.6) | collective-permute-done | bytes 262176 | tf_op jit(solution)/shard_map/ppermute | solution.py:51
  88.3 8.3 %collective-permute-done.8 = bf16[4,2,128,128]{3,2,1,0:T(8,128)(2,1)} collective-permute-done((bf16[4,2,128,128]{3,2,1,0:T(8,128)(2,1)}, bf16[4,2,128,128]{3,2,1,0:T(8,128)(2,1)}, u32[]{:S(2)}, u32[]{:S(2)}) %collective-permute-start.8) | collective-permute-done | bytes 262176 | tf_op jit(solution)/shard_map/ppermute | solution.py:51
  102.9 5.1 %collective-permute-done.1 = f32[2,128,128]{2,1,0:T(8,128)} collective-permute-done((f32[2,128,128]{2,1,0:T(8,128)}, f32[2,128,128]{2,1,0:T(8,128)}, u32[]{:S(2)}, u32[]{:S(2)}) %collective-permute-start.1) | collective-permute-done | bytes 131104 | tf_op jit(solution)/shard_map/ppermute | solution.py:42
  140.6 4.4 %collective-permute-done.15 = bf16[1,96,2048]{2,1,0:T(8,128)(2,1)S(1)} collective-permute-done((bf16[1,96,2048]{2,1,0:T(8,128)(2,1)S(1)}, bf16[1,96,2048]{2,1,0:T(8,128)(2,1)S(1)}, u32[]{:S(2)}, u32[]{:S(2)}) %collective-permute-start.15) | collective-permute-done | bytes 393248 | tf_op jit(solution)/shard_map/ppermute | solution.py:32
  149.0 24.0 %collective-permute-done.16 = bf16[1,96,2048]{2,1,0:T(8,128)(2,1)S(1)} collective-permute-done((bf16[1,96,2048]{2,1,0:T(8,128)(2,1)S(1)}, bf16[1,96,2048]{2,1,0:T(8,128)(2,1)S(1)}, u32[]{:S(2)}, u32[]{:S(2)}) %collective-permute-start.16) | collective-permute-done | bytes 393248 | tf_op jit(solution)/shard_map/ppermute | solution.py:32
  179.4 4.5 %collective-permute-start.24 = (bf16[1,96,2048]{2,1,0:T(8,128)(2,1)S(1)}, bf16[1,96,2048]{2,1,0:T(8,128)(2,1)S(1)}, u32[]{:S(2)}, u32[]{:S(2)}) collective-permute-start(bf16[1,96,2048]{2,1,0:T(8,128)(2,1)S(1)} %get-tuple-element.12), channel_id=1, source_target_pairs={{0,10},{1,11},{2,8},{3,9},{4,14},{5,15},{6,12},{7,13},{8,2},{9,3},... | collective-permute-start | bytes 1179656 | tf_op jit(solution)/shard_map/ppermute | solution.py:32
  195.7 6.2 %collective-permute-done.23 = bf16[1,96,2048]{2,1,0:T(8,128)(2,1)S(1)} collective-permute-done((bf16[1,96,2048]{2,1,0:T(8,128)(2,1)S(1)}, bf16[1,96,2048]{2,1,0:T(8,128)(2,1)S(1)}, u32[]{:S(2)}, u32[]{:S(2)}) %collective-permute-start.23) | collective-permute-done | bytes 393248 | tf_op jit(solution)/shard_map/ppermute | solution.py:32
  201.9 4.4 %collective-permute-start.28 = (bf16[1,96,2048]{2,1,0:T(8,128)(2,1)S(1)}, bf16[1,96,2048]{2,1,0:T(8,128)(2,1)S(1)}, u32[]{:S(2)}, u32[]{:S(2)}) collective-permute-start(bf16[1,96,2048]{2,1,0:T(8,128)(2,1)S(1)} %get-tuple-element.8), channel_id=1, source_target_pairs={{0,14},{1,15},{2,12},{3,13},{4,10},{5,11},{6,8},{7,9},{8,6},{9,7},... | collective-permute-start | bytes 1179656 | tf_op jit(solution)/shard_map/ppermute | solution.py:32
  210.5 3.7 collective-permute-start.29
  214.9 5.4 %collective-permute-done.25 = bf16[1,96,2048]{2,1,0:T(8,128)(2,1)S(1)} collective-permute-done((bf16[1,96,2048]{2,1,0:T(8,128)(2,1)S(1)}, bf16[1,96,2048]{2,1,0:T(8,128)(2,1)S(1)}, u32[]{:S(2)}, u32[]{:S(2)}) %collective-permute-start.25) | collective-permute-done | bytes 393248 | tf_op jit(solution)/shard_map/ppermute | solution.py:32
  221.0 5.0 %collective-permute-done.26 = bf16[1,96,2048]{2,1,0:T(8,128)(2,1)S(1)} collective-permute-done((bf16[1,96,2048]{2,1,0:T(8,128)(2,1)S(1)}, bf16[1,96,2048]{2,1,0:T(8,128)(2,1)S(1)}, u32[]{:S(2)}, u32[]{:S(2)}) %collective-permute-start.26) | collective-permute-done | bytes 393248 | tf_op jit(solution)/shard_map/ppermute | solution.py:32
  226.8 7.9 %collective-permute-done.27 = bf16[1,96,2048]{2,1,0:T(8,128)(2,1)S(1)} collective-permute-done((bf16[1,96,2048]{2,1,0:T(8,128)(2,1)S(1)}, bf16[1,96,2048]{2,1,0:T(8,128)(2,1)S(1)}, u32[]{:S(2)}, u32[]{:S(2)}) %collective-permute-start.27) | collective-permute-done | bytes 393248 | tf_op jit(solution)/shard_map/ppermute | solution.py:32
  235.5 8.0 %collective-permute-done.28 = bf16[1,96,2048]{2,1,0:T(8,128)(2,1)S(1)} collective-permute-done((bf16[1,96,2048]{2,1,0:T(8,128)(2,1)S(1)}, bf16[1,96,2048]{2,1,0:T(8,128)(2,1)S(1)}, u32[]{:S(2)}, u32[]{:S(2)}) %collective-permute-start.28) | collective-permute-done | bytes 393248 | tf_op jit(solution)/shard_map/ppermute | solution.py:32
  244.3 9.9 %collective-permute-done.29 = bf16[1,96,2048]{2,1,0:T(8,128)(2,1)S(1)} collective-permute-done((bf16[1,96,2048]{2,1,0:T(8,128)(2,1)S(1)}, bf16[1,96,2048]{2,1,0:T(8,128)(2,1)S(1)}, u32[]{:S(2)}, u32[]{:S(2)}) %collective-permute-start.29) | collective-permute-done | bytes 393248 | tf_op jit(solution)/shard_map/ppermute | solution.py:32
  255.1 6.4 %gather_fusion = bf16[16,96,2048]{2,1,0:T(8,128)(2,1)} fusion(bf16[16,96,2048]{2,1,0:T(8,128)(2,1)} %bitcast.53, s32[1024]{0:T(1024)S(1)} %pad_clamp_fusion), kind=kCustom, calls=%fused_computation | custom fusion | bytes 12582976 | tf_op jit(solution)/shard_map/gather | solution.py:33
  261.4 17.6 %fusion = f32[1536,2048]{1,0:T(8,128)S(1)} fusion(bf16[1536,2048]{1,0:T(8,128)(2,1)} %bitcast.119, bf16[1,2048,2048]{2,1,0:T(8,128)(2,1)} %param.14), kind=kOutput, calls=%fused_computation.1 | convolution fusion | flops 12884901888 | bytes 27262976 | tf_op jit(solution)/shard_map/dot_general | solution.py:149
  279.1 8.7 %convolution_convert_fusion.1 = bf16[1536,2048]{1,0:T(8,128)(2,1)} fusion(bf16[1,1024,2048]{2,1,0:T(8,128)(2,1)S(1)} %copy-done.3, f32[1536,2048]{1,0:T(8,128)S(1)} %fusion), kind=kOutput, calls=%fused_computation.4 | convolution fusion | flops 6455033856 | bytes 23068672 | tf_op jit(solution)/shard_map/dot_general | solution.py:151
  287.7 7.1 %all-to-all-start.1 = ((bf16[16,96,2048]{2,1,0:T(8,128)(2,1)}), bf16[16,96,2048]{2,1,0:T(8,128)(2,1)}, u32[]{:S(2)}, u32[]{:S(2)}) async-start(bf16[16,96,2048]{2,1,0:T(8,128)(2,1)} %bitcast.118), calls=%async_computation.1 | async-start | bytes 12582912 | tf_op jit(solution)/shard_map/all_to_all | solution.py:152
  295.1 108.7 %all-to-all-done.1 = bf16[16,96,2048]{2,1,0:T(8,128)(2,1)} async-done(((bf16[16,96,2048]{2,1,0:T(8,128)(2,1)}), bf16[16,96,2048]{2,1,0:T(8,128)(2,1)}, u32[]{:S(2)}, u32[]{:S(2)}) %all-to-all-start.1) | async-done | bytes 6291488 | tf_op jit(solution)/shard_map/all_to_all | solution.py:152
  403.9 5.5 %fusion.20 = f32[512,2048]{1,0:T(8,128)S(1)} fusion(bf16[1536,2048]{1,0:T(8,128)(2,1)} %bitcast.59, bf16[256,1536]{0,1:T(8,128)(2,1)S(1)} %get-tuple-element.41, bf16[256,1536]{0,1:T(8,128)(2,1)S(1)} %get-tuple-element.40), kind=kOutput, calls=%fused_computation.31 | convolution fusion | flops 3224371200 | bytes 12058624 | tf_op jit(solution)/shard_map/dot_general | solution.py:155
  (113 shorter events, 86.7 us)
Async XLA Ops:
  6.5 119.1 %all-gather.2.cloned.1.call-start = ((), (), s32[]{:S(2)}) async-start(), calls=%async_computation.2 | async-start | bytes 4456448 | tf_op jit(solution)/shard_map/all_gather | solution.py:97
  10.3 53.1 %all-to-all-start = ((bf16[16,128,768]{2,1,0:T(8,128)(2,1)}), bf16[16,128,768]{2,1,0:T(8,128)(2,1)}, u32[]{:S(2)}, u32[]{:S(2)}) async-start(bf16[16,128,768]{2,1,0:T(8,128)(2,1)} %broadcast_in_dim.78), calls=%async_computation | async-start | bytes 6291456 | tf_op jit(solution)/shard_map/all_to_all | solution.py:57
  18.0 24.4 %collective-permute-start.4 = (bf16[256,2048]{1,0:T(8,128)(2,1)S(1)}, bf16[256,2048]{1,0:T(8,128)(2,1)S(1)}, u32[]{:S(2)}, u32[]{:S(2)}) collective-permute-start(bf16[256,2048]{1,0:T(8,128)(2,1)S(1)} %fusion.16), channel_id=1, source_target_pairs={{0,32},{16,48},{32,0},{48,16},{64,96},{80,112},{96,64},{112,80},{1... | collective-permute-start | bytes 3145736 | tf_op jit(solution)/shard_map/ppermute | solution.py:42
  18.5 23.9 %collective-permute-start.3 = (bf16[256,2048]{1,0:T(8,128)(2,1)S(1)}, bf16[256,2048]{1,0:T(8,128)(2,1)S(1)}, u32[]{:S(2)}, u32[]{:S(2)}) collective-permute-start(bf16[256,2048]{1,0:T(8,128)(2,1)S(1)} %fusion.16), channel_id=1, source_target_pairs={{0,16},{16,0},{32,48},{48,32},{64,80},{80,64},{96,112},{112,96},{1... | collective-permute-start | bytes 3145736 | tf_op jit(solution)/shard_map/ppermute | solution.py:42
  71.7 15.0 %collective-permute-start.6 = (bf16[4,2,128,128]{3,2,1,0:T(8,128)(2,1)}, bf16[4,2,128,128]{3,2,1,0:T(8,128)(2,1)S(1)}, u32[]{:S(2)}, u32[]{:S(2)}) collective-permute-start(bf16[4,2,128,128]{3,2,1,0:T(8,128)(2,1)} %get-tuple-element.42), channel_id=1, source_target_pairs={{0,1},{1,2},{2,3},{3,0},{4,5},{5,6},{6,7},{7,4},{8,9},{9,10},{10,1... | collective-permute-start | bytes 786440 | tf_op jit(solution)/shard_map/ppermute | solution.py:51
  71.7 16.6 %collective-permute-start.7 = (bf16[4,2,128,128]{3,2,1,0:T(8,128)(2,1)}, bf16[4,2,128,128]{3,2,1,0:T(8,128)(2,1)}, u32[]{:S(2)}, u32[]{:S(2)}) collective-permute-start(bf16[4,2,128,128]{3,2,1,0:T(8,128)(2,1)} %get-tuple-element.42), channel_id=1, source_target_pairs={{0,2},{1,3},{2,0},{3,1},{4,6},{5,7},{6,4},{7,5},{8,10},{9,11},{10,... | collective-permute-start | bytes 786440 | tf_op jit(solution)/shard_map/ppermute | solution.py:51
  73.7 22.9 %collective-permute-start.8 = (bf16[4,2,128,128]{3,2,1,0:T(8,128)(2,1)}, bf16[4,2,128,128]{3,2,1,0:T(8,128)(2,1)}, u32[]{:S(2)}, u32[]{:S(2)}) collective-permute-start(bf16[4,2,128,128]{3,2,1,0:T(8,128)(2,1)} %get-tuple-element.42), channel_id=1, source_target_pairs={{0,3},{1,0},{2,1},{3,2},{4,7},{5,4},{6,5},{7,6},{8,11},{9,8},{10,9... | collective-permute-start | bytes 786440 | tf_op jit(solution)/shard_map/ppermute | solution.py:51
  75.6 26.3 %collective-permute-start = (f32[2,128,128]{2,1,0:T(8,128)S(1)}, f32[2,128,128]{2,1,0:T(8,128)}, u32[]{:S(2)}, u32[]{:S(2)}) collective-permute-start(f32[2,128,128]{2,1,0:T(8,128)S(1)} %get-tuple-element.37), channel_id=1, source_target_pairs={{0,16},{16,0},{32,48},{48,32},{64,80},{80,64},{96,112},{112,96},{1... | collective-permute-start | bytes 393224 | tf_op jit(solution)/shard_map/ppermute | solution.py:42
  133.1 11.9 %collective-permute-start.15 = (bf16[1,96,2048]{2,1,0:T(8,128)(2,1)S(1)}, bf16[1,96,2048]{2,1,0:T(8,128)(2,1)S(1)}, u32[]{:S(2)}, u32[]{:S(2)}) collective-permute-start(bf16[1,96,2048]{2,1,0:T(8,128)(2,1)S(1)} %get-tuple-element.21), channel_id=1, source_target_pairs={{0,1},{1,0},{2,3},{3,2},{4,5},{5,4},{6,7},{7,6},{8,9},{9,8},{10,11... | collective-permute-start | bytes 1179656 | tf_op jit(solution)/shard_map/ppermute | solution.py:32
  135.5 37.4 %collective-permute-start.16 = (bf16[1,96,2048]{2,1,0:T(8,128)(2,1)S(1)}, bf16[1,96,2048]{2,1,0:T(8,128)(2,1)S(1)}, u32[]{:S(2)}, u32[]{:S(2)}) collective-permute-start(bf16[1,96,2048]{2,1,0:T(8,128)(2,1)S(1)} %get-tuple-element.20), channel_id=1, source_target_pairs={{0,2},{1,3},{2,0},{3,1},{4,6},{5,7},{6,4},{7,5},{8,10},{9,11},{10,... | collective-permute-start | bytes 1179656 | tf_op jit(solution)/shard_map/ppermute | solution.py:32
  138.0 36.4 %collective-permute-start.17 = (bf16[1,96,2048]{2,1,0:T(8,128)(2,1)S(1)}, bf16[1,96,2048]{2,1,0:T(8,128)(2,1)S(1)}, u32[]{:S(2)}, u32[]{:S(2)}) collective-permute-start(bf16[1,96,2048]{2,1,0:T(8,128)(2,1)S(1)} %get-tuple-element.19), channel_id=1, source_target_pairs={{0,3},{1,2},{2,1},{3,0},{4,7},{5,6},{6,5},{7,4},{8,11},{9,10},{10,... | collective-permute-start | bytes 1179656 | tf_op jit(solution)/shard_map/ppermute | solution.py:32
  138.3 37.8 %collective-permute-start.18 = (bf16[1,96,2048]{2,1,0:T(8,128)(2,1)S(1)}, bf16[1,96,2048]{2,1,0:T(8,128)(2,1)S(1)}, u32[]{:S(2)}, u32[]{:S(2)}) collective-permute-start(bf16[1,96,2048]{2,1,0:T(8,128)(2,1)S(1)} %get-tuple-element.18), channel_id=1, source_target_pairs={{0,4},{1,5},{2,6},{3,7},{4,0},{5,1},{6,2},{7,3},{8,12},{9,13},{10,... | collective-permute-start | bytes 1179656 | tf_op jit(solution)/shard_map/ppermute | solution.py:32
  139.5 39.9 %collective-permute-start.19 = (bf16[1,96,2048]{2,1,0:T(8,128)(2,1)S(1)}, bf16[1,96,2048]{2,1,0:T(8,128)(2,1)S(1)}, u32[]{:S(2)}, u32[]{:S(2)}) collective-permute-start(bf16[1,96,2048]{2,1,0:T(8,128)(2,1)S(1)} %get-tuple-element.17), channel_id=1, source_target_pairs={{0,5},{1,4},{2,7},{3,6},{4,1},{5,0},{6,3},{7,2},{8,13},{9,12},{10,... | collective-permute-start | bytes 1179656 | tf_op jit(solution)/shard_map/ppermute | solution.py:32
  145.0 39.7 %collective-permute-start.20 = (bf16[1,96,2048]{2,1,0:T(8,128)(2,1)S(1)}, bf16[1,96,2048]{2,1,0:T(8,128)(2,1)S(1)}, u32[]{:S(2)}, u32[]{:S(2)}) collective-permute-start(bf16[1,96,2048]{2,1,0:T(8,128)(2,1)S(1)} %get-tuple-element.16), channel_id=1, source_target_pairs={{0,6},{1,7},{2,4},{3,5},{4,2},{5,3},{6,0},{7,1},{8,14},{9,15},{10,... | collective-permute-start | bytes 1179656 | tf_op jit(solution)/shard_map/ppermute | solution.py:32
  173.0 14.6 %collective-permute-start.21 = (bf16[1,96,2048]{2,1,0:T(8,128)(2,1)S(1)}, bf16[1,96,2048]{2,1,0:T(8,128)(2,1)S(1)}, u32[]{:S(2)}, u32[]{:S(2)}) collective-permute-start(bf16[1,96,2048]{2,1,0:T(8,128)(2,1)S(1)} %get-tuple-element.15), channel_id=1, source_target_pairs={{0,7},{1,6},{2,5},{3,4},{4,3},{5,2},{6,1},{7,0},{8,15},{9,14},{10,... | collective-permute-start | bytes 1179656 | tf_op jit(solution)/shard_map/ppermute | solution.py:32
  174.4 18.6 %collective-permute-start.22 = (bf16[1,96,2048]{2,1,0:T(8,128)(2,1)S(1)}, bf16[1,96,2048]{2,1,0:T(8,128)(2,1)S(1)}, u32[]{:S(2)}, u32[]{:S(2)}) collective-permute-start(bf16[1,96,2048]{2,1,0:T(8,128)(2,1)S(1)} %get-tuple-element.14), channel_id=1, source_target_pairs={{0,8},{1,9},{2,10},{3,11},{4,12},{5,13},{6,14},{7,15},{8,0},{9,1},... | collective-permute-start | bytes 1179656 | tf_op jit(solution)/shard_map/ppermute | solution.py:32
  176.1 25.8 %collective-permute-start.23 = (bf16[1,96,2048]{2,1,0:T(8,128)(2,1)S(1)}, bf16[1,96,2048]{2,1,0:T(8,128)(2,1)S(1)}, u32[]{:S(2)}, u32[]{:S(2)}) collective-permute-start(bf16[1,96,2048]{2,1,0:T(8,128)(2,1)S(1)} %get-tuple-element.13), channel_id=1, source_target_pairs={{0,9},{1,8},{2,11},{3,10},{4,13},{5,12},{6,15},{7,14},{8,1},{9,0},... | collective-permute-start | bytes 1179656 | tf_op jit(solution)/shard_map/ppermute | solution.py:32
  179.4 31.0 %collective-permute-start.24 = (bf16[1,96,2048]{2,1,0:T(8,128)(2,1)S(1)}, bf16[1,96,2048]{2,1,0:T(8,128)(2,1)S(1)}, u32[]{:S(2)}, u32[]{:S(2)}) collective-permute-start(bf16[1,96,2048]{2,1,0:T(8,128)(2,1)S(1)} %get-tuple-element.12), channel_id=1, source_target_pairs={{0,10},{1,11},{2,8},{3,9},{4,14},{5,15},{6,12},{7,13},{8,2},{9,3},... | collective-permute-start | bytes 1179656 | tf_op jit(solution)/shard_map/ppermute | solution.py:32
  184.7 35.5 %collective-permute-start.25 = (bf16[1,96,2048]{2,1,0:T(8,128)(2,1)S(1)}, bf16[1,96,2048]{2,1,0:T(8,128)(2,1)S(1)}, u32[]{:S(2)}, u32[]{:S(2)}) collective-permute-start(bf16[1,96,2048]{2,1,0:T(8,128)(2,1)S(1)} %get-tuple-element.11), channel_id=1, source_target_pairs={{0,11},{1,10},{2,9},{3,8},{4,15},{5,14},{6,13},{7,12},{8,3},{9,2},... | collective-permute-start | bytes 1179656 | tf_op jit(solution)/shard_map/ppermute | solution.py:32
  187.6 38.5 %collective-permute-start.26 = (bf16[1,96,2048]{2,1,0:T(8,128)(2,1)S(1)}, bf16[1,96,2048]{2,1,0:T(8,128)(2,1)S(1)}, u32[]{:S(2)}, u32[]{:S(2)}) collective-permute-start(bf16[1,96,2048]{2,1,0:T(8,128)(2,1)S(1)} %get-tuple-element.10), channel_id=1, source_target_pairs={{0,12},{1,13},{2,14},{3,15},{4,8},{5,9},{6,10},{7,11},{8,4},{9,5},... | collective-permute-start | bytes 1179656 | tf_op jit(solution)/shard_map/ppermute | solution.py:32
  193.0 41.8 %collective-permute-start.27 = (bf16[1,96,2048]{2,1,0:T(8,128)(2,1)S(1)}, bf16[1,96,2048]{2,1,0:T(8,128)(2,1)S(1)}, u32[]{:S(2)}, u32[]{:S(2)}) collective-permute-start(bf16[1,96,2048]{2,1,0:T(8,128)(2,1)S(1)} %get-tuple-element.9), channel_id=1, source_target_pairs={{0,13},{1,12},{2,15},{3,14},{4,9},{5,8},{6,11},{7,10},{8,5},{9,4},... | collective-permute-start | bytes 1179656 | tf_op jit(solution)/shard_map/ppermute | solution.py:32
  201.9 41.6 %collective-permute-start.28 = (bf16[1,96,2048]{2,1,0:T(8,128)(2,1)S(1)}, bf16[1,96,2048]{2,1,0:T(8,128)(2,1)S(1)}, u32[]{:S(2)}, u32[]{:S(2)}) collective-permute-start(bf16[1,96,2048]{2,1,0:T(8,128)(2,1)S(1)} %get-tuple-element.8), channel_id=1, source_target_pairs={{0,14},{1,15},{2,12},{3,13},{4,10},{5,11},{6,8},{7,9},{8,6},{9,7},... | collective-permute-start | bytes 1179656 | tf_op jit(solution)/shard_map/ppermute | solution.py:32
  210.5 43.8 %collective-permute-start.29 = (bf16[1,96,2048]{2,1,0:T(8,128)(2,1)S(1)}, bf16[1,96,2048]{2,1,0:T(8,128)(2,1)S(1)}, u32[]{:S(2)}, u32[]{:S(2)}) collective-permute-start(bf16[1,96,2048]{2,1,0:T(8,128)(2,1)S(1)} %get-tuple-element.7), channel_id=1, source_target_pairs={{0,15},{1,14},{2,13},{3,12},{4,11},{5,10},{6,9},{7,8},{8,7},{9,6},... | collective-permute-start | bytes 1179656 | tf_op jit(solution)/shard_map/ppermute | solution.py:32
  287.7 116.1 %all-to-all-start.1 = ((bf16[16,96,2048]{2,1,0:T(8,128)(2,1)}), bf16[16,96,2048]{2,1,0:T(8,128)(2,1)}, u32[]{:S(2)}, u32[]{:S(2)}) async-start(bf16[16,96,2048]{2,1,0:T(8,128)(2,1)} %bitcast.118), calls=%async_computation.1 | async-start | bytes 12582912 | tf_op jit(solution)/shard_map/all_to_all | solution.py:152
  (14 other events, 134.6 us)
Sparse Core Ops, SparseCore 0:
  9.5 89.8 all-gather.1
